TPU v7x, 256 devices: a whole 4x4x8 slice. The times are simulated.
256 devices in a mesh: ta: 4 (over y), ha: 16 (over x, z_hi, core), wa: 4 (over z_lo).
Axes of the slice: x: 4, y: 4, z: 8 (z_hi: 2, z_lo: 4; z = z_hi * 4 + z_lo), core: 2. Of those that a mesh axis runs over, the one named last changes fastest.
Arguments:
- latents: bfloat16 [8, 256, 128, 256], P('ta', 'ha', 'wa'), may hold values from -6 to 6
- norm_gain: float32 [256], replicated, may hold values from 0.1 to 1.9
- conv_weight: bfloat16 [3, 3, 3, 256, 256], replicated, may hold values from -0.078125 to 0.078125
- qkv_weight: bfloat16 [1024, 16, 3, 128], P(None, ('ta', 'wa')), may hold values from -2.7 to 2.7
Outputs:
- block_out: bfloat16 [8, 256, 128, 256], P('ta', 'ha', 'wa')
- attended: bfloat16 [8, 128, 64, 16, 128], P(None, 'ha', None, ('ta', 'wa'))
All inputs are finite; a program needn't handle non-finite values.
Results may differ from a plain program's by a relative error of at most 0.0062.
Values may be sent and summed in bfloat16 or wider, within the bound.
No kernel may reach another device: no remote copies, remote signals or barrier semaphores. Data moves between devices by JAX's collectives and lax.ppermute only.
A program may use at most 128 MiB of HBM per device.

v0:
```python
import jax
import jax.numpy as jnp
from jax import lax
from jax.sharding import PartitionSpec as P

WIN = 4


def extended(cells, sides, width):
    for axis, dim in sides:
        count = lax.axis_size(axis)
        ends = count - 1
        head = lax.slice_in_dim(cells, 0, width, axis=dim)
        tail = lax.slice_in_dim(cells, cells.shape[dim] - width, cells.shape[dim], axis=dim)
        cells = jnp.concatenate(
            [
                lax.ppermute(tail, axis, [(i, (i + 1) % count) for i in range(ends)]),
                cells,
                lax.ppermute(head, axis, [((i + 1) % count, i) for i in range(ends)]),
            ],
            axis=dim,
        )
    return cells


def local(latents, norm_gain, conv_weight, qkv_weight):
    t_dev, h_dev, w_dev, channels = latents.shape
    rows_dev = h_dev // 2
    cols_dev = w_dev // 2
    latent_f32 = latents.astype(jnp.float32)
    scale_rms = lax.rsqrt(jnp.mean(latent_f32 * latent_f32, axis=-1, keepdims=True) + 1e-06)
    normed = jax.nn.silu(latent_f32 * scale_rms * norm_gain).astype(jnp.bfloat16)
    padded = extended(normed, (("ta", 0), ("ha", 1), ("wa", 2)), 1)
    conv_out = lax.conv_general_dilated(
        padded[None],
        conv_weight,
        (1, 1, 1),
        "VALID",
        dimension_numbers=("NDHWC", "DHWIO", "NDHWC"),
        preferred_element_type=jnp.float32,
    )[0]
    block_out = (latent_f32 + conv_out).astype(jnp.bfloat16)
    width_in, head_dev, qkv_count, head_size = qkv_weight.shape
    col_heads = lax.all_gather(qkv_weight, "ta", axis=1, tiled=True)
    heads = col_heads.shape[1]
    wide = lax.all_gather(block_out, "wa", axis=2, tiled=True)
    patch_cols = wide.shape[2] // 2
    patches = (
        wide.reshape(t_dev, rows_dev, 2, patch_cols, 2, channels)
        .transpose(0, 1, 3, 2, 4, 5)
        .reshape(t_dev * rows_dev * patch_cols, 4 * channels)
    )
    projected = jnp.dot(
        patches, col_heads.reshape(width_in, -1), preferred_element_type=jnp.float32
    ).astype(jnp.bfloat16)
    qkv_rows = projected.reshape(t_dev, rows_dev, patch_cols, heads, qkv_count, head_size)
    queries = qkv_rows[:, :, :, :, 0, :]
    key_value = qkv_rows[:, :, :, :, 1:, :].reshape(
        t_dev, rows_dev, patch_cols, heads, 2 * head_size
    )
    kv_rim = extended(key_value, (("ha", 1),), WIN)
    row_base = lax.axis_index("ha") * rows_dev
    total_rows = rows_dev * lax.axis_size("ha")

    def attend(block_idx):
        q_block = lax.dynamic_slice_in_dim(queries, block_idx * WIN, WIN, 1)
        kv_block = lax.dynamic_slice_in_dim(kv_rim, block_idx * WIN, 3 * WIN, 1)
        key_part = kv_block[..., :head_size]
        value_part = kv_block[..., head_size:]
        scores = jnp.einsum(
            "tiahd,tjbhd->thiajb", q_block, key_part, preferred_element_type=jnp.float32
        ) * head_size ** (-0.5)
        q_row = jnp.arange(WIN, dtype=jnp.int32)[:, None]
        k_row = jnp.arange(3 * WIN, dtype=jnp.int32)[None, :] - WIN
        k_global = row_base + block_idx * WIN + k_row
        allowed = (jnp.abs(q_row - k_row) <= WIN) & (k_global >= 0) & (k_global < total_rows)
        scores = jnp.where(allowed[None, None, :, None, :, None], scores, -1e30)
        row_max = jnp.max(scores, axis=(4, 5), keepdims=True)
        exp_scores = jnp.exp(scores - row_max)
        probs = (exp_scores / jnp.sum(exp_scores, axis=(4, 5), keepdims=True)).astype(jnp.bfloat16)
        result = jnp.einsum(
            "thiajb,tjbhd->tiahd", probs, value_part, preferred_element_type=jnp.float32
        )
        return result.astype(jnp.bfloat16)

    blocks = lax.map(attend, jnp.arange(rows_dev // WIN, dtype=jnp.int32))
    attended = blocks.transpose(1, 0, 2, 3, 4, 5).reshape(
        t_dev, rows_dev, patch_cols, heads, head_size
    )
    attended = lax.all_to_all(attended, "ta", split_axis=3, concat_axis=0, tiled=True)
    return (block_out, attended)


def solution(mesh):
    return jax.shard_map(
        local,
        mesh=mesh,
        in_specs=(P("ta", "ha", "wa", None), P(), P(), P(None, ("ta", "wa"), None, None)),
        out_specs=(P("ta", "ha", "wa", None), P(None, "ha", None, ("ta", "wa"), None)),
        check_vma=False,
    )
```

profile of v0, /device:TPU:67, one launch (start us, length us, event | category | flops | bytes accessed | tf_op | source)
XLA Modules:
  0.0 310.4 jit_solution(17546351096016199151)
XLA Ops:
  10.4 3.2 %collective-permute-start = (bf16[1,16,32,256]{3,1,2,0:T(8,128)(2,1)S(1)}, bf16[1,16,32,256]{3,1,2,0:T(8,128)(2,1)S(1)}, u32[]{:S(2)}, u32[]{:S(2)}) collective-permute-start(bf16[1,16,32,256]{3,1,2,0:T(8,128)(2,1)S(1)} %get-tuple-element.126), channel_id=1, source_target_pairs={{0,64},{64,128},{128,192},{1,65},{65,129},{129,193},{2,66},{66,130... | collective-permute-start | bytes 786440 | tf_op jit(solution)/shard_map/ppermute | solution.py:17
  14.9 3.7 %collective-permute-done = bf16[1,16,32,256]{3,1,2,0:T(8,128)(2,1)S(1)} collective-permute-done((bf16[1,16,32,256]{3,1,2,0:T(8,128)(2,1)S(1)}, bf16[1,16,32,256]{3,1,2,0:T(8,128)(2,1)S(1)}, u32[]{:S(2)}, u32[]{:S(2)}) %collective-permute-start) | collective-permute-done | bytes 262176 | tf_op jit(solution)/shard_map/ppermute | solution.py:17
  18.6 3.8 %collective-permute-done.1 = bf16[1,16,32,256]{3,1,2,0:T(8,128)(2,1)S(1)} collective-permute-done((bf16[1,16,32,256]{3,1,2,0:T(8,128)(2,1)S(1)}, bf16[1,16,32,256]{3,1,2,0:T(8,128)(2,1)S(1)}, u32[]{:S(2)}, u32[]{:S(2)}) %collective-permute-start.1) | collective-permute-done | bytes 262176 | tf_op jit(solution)/shard_map/ppermute | solution.py:19
  22.6 8.7 %collective-permute-start.2 = (bf16[4,1,32,256]{3,1,2,0:T(2,128)(2,1)S(1)}, bf16[4,1,32,256]{3,1,2,0:T(2,128)(2,1)S(1)}, u32[]{:S(2)}, u32[]{:S(2)}) collective-permute-start(bf16[4,1,32,256]{3,1,2,0:T(2,128)(2,1)S(1)} %get-tuple-element.124), channel_id=1, source_target_pairs={{0,4},{4,8},{8,12},{12,16},{16,20},{20,24},{24,28},{28,32},{32,36}... | collective-permute-start | bytes 196616 | tf_op jit(solution)/shard_map/ppermute | solution.py:17
  33.9 9.1 %collective-permute-done.3 = bf16[4,1,32,256]{3,1,2,0:T(2,128)(2,1)S(1)} collective-permute-done((bf16[4,1,32,256]{3,1,2,0:T(2,128)(2,1)S(1)}, bf16[4,1,32,256]{3,1,2,0:T(2,128)(2,1)S(1)}, u32[]{:S(2)}, u32[]{:S(2)}) %collective-permute-start.3) | collective-permute-done | bytes 65568 | tf_op jit(solution)/shard_map/ppermute | solution.py:19
  44.9 3.4 %collective-permute-start.5 = (bf16[4,18,1,256]{3,1,2,0:T(8,128)(2,1)S(1)}, bf16[4,18,1,256]{3,1,2,0:T(8,128)(2,1)S(1)}, u32[]{:S(2)}, u32[]{:S(2)}) collective-permute-start(bf16[4,18,1,256]{3,1,2,0:T(8,128)(2,1)S(1)} %get-tuple-element.123), channel_id=1, source_target_pairs={{1,0},{2,1},{3,2},{5,4},{6,5},{7,6},{9,8},{10,9},{11,10},{13,12},{... | collective-permute-start | bytes 110600 | tf_op jit(solution)/shard_map/ppermute | solution.py:19
  52.6 5.0 %fusion.23 = f32[2,16,8,5,256]{4,2,3,1,0:T(8,128)S(1)} fusion(bf16[3,3,3,256,256]{4,3,2,1,0:T(8,128)(2,1)S(1)} %copy-done, bf16[4,18,1,7,2,256]{5,3,4,1,0,2:T(8,128)(2,1)S(1)} %slice.56, bf16[4,18,1,8,5,256]{5,3,4,1,0,2:T(8,128)(2,1)S(1)} %copy.44, pred[8,5]{0,1:T(8,128)(4,1)S(1)} %copy-done.6), kind=kOutput, calls=%fused_computation.40 | convolution fusion | flops 4536369152 | bytes 6840360 | tf_op jit(solution)/shard_map/conv_general_dilated | solution.py:34
  60.0 46.3 %all-gather.3.cloned.1.call-done = bf16[2,16,128,256]{3,1,2,0:T(8,128)(2,1)} async-done(((bf16[2,16,32,256]{3,1,2,0:T(8,128)(2,1)}), bf16[2,16,128,256]{3,1,2,0:T(8,128)(2,1)}) %all-gather.3.cloned.1.call-update) | async-done | bytes 2097168 | tf_op jit(solution)/shard_map/all_gather | solution.py:46
  106.3 2.7 reshape.104
  109.0 3.5 %copy.74 = bf16[2,8,2,64,2,256]{5,4,2,3,1,0:T(2,128)(2,1)} copy(bf16[2,8,2,64,2,256]{5,2,1,4,3,0:T(2,128)(2,1)S(1)} %reshape.104) | data formatting | bytes 4194304 | tf_op jit(solution)/shard_map/reshape | solution.py:49
  112.6 4.5 %reshape.105 = bf16[1024,1024]{1,0:T(8,128)(2,1)} reshape(bf16[2,8,64,2,2,256]{5,4,3,2,1,0:T(2,128)(2,1)} %bitcast.88) | data formatting | bytes 4194304 | tf_op jit(solution)/shard_map/reshape | solution.py:51
  117.0 33.7 %all-gather.5.cloned.1.call-done = bf16[1024,4,3,128]{3,0,2,1:T(8,128)(2,1)} async-done(((bf16[1024,1,3,128]{3,0,2,1:T(8,128)(2,1)}), bf16[1024,4,3,128]{3,0,2,1:T(8,128)(2,1)}) %all-gather.5.cloned.1.call-update) | async-done | bytes 3145744 | tf_op jit(solution)/shard_map/all_gather | solution.py:44
  150.7 4.6 %copy.47 = bf16[1024,4,3,128]{0,3,2,1:T(8,128)(2,1)} copy(bf16[1024,4,3,128]{3,0,2,1:T(8,128)(2,1)} %all-gather.5.cloned.1.call-done) | data formatting | bytes 6291456 | tf_op jit(solution)/shard_map/all_gather | solution.py:44
  155.4 6.0 %convolution_convert_fusion = bf16[1024,1536]{1,0:T(8,128)(2,1)S(1)} fusion(bf16[1024,1024]{1,0:T(8,128)(2,1)} %reshape.105, bf16[1024,1536]{0,1:T(8,128)(2,1)} %bitcast.91), kind=kOutput, calls=%fused_computation.28 | convolution fusion | flops 3222798336 | bytes 8388608 | tf_op jit(solution)/shard_map/dot_general | solution.py:53
  161.3 4.5 %reshape.107 = bf16[2,8,64,4,3,128]{5,4,3,2,1,0:T(4,128)(2,1)} reshape(bf16[1024,1536]{1,0:T(8,128)(2,1)S(1)} %convolution_convert_fusion) | data formatting | bytes 6291456 | tf_op jit(solution)/shard_map/reshape | solution.py:56
  165.9 4.6 %slice.58 = bf16[2,8,64,4,2,128]{5,4,3,2,1,0:T(2,128)(2,1)S(1)} slice(bf16[2,8,64,4,3,128]{5,4,3,2,1,0:T(4,128)(2,1)} %reshape.107), slice={[0:2], [0:8], [0:64], [0:4], [1:3], [0:128]} | slice | bytes 4194304 | tf_op jit(solution)/shard_map/slice | solution.py:58
  176.7 6.3 %collective-permute-start.6 = (bf16[2,4,64,4,256]{4,2,1,3,0:T(8,128)(2,1)}, bf16[2,4,64,4,256]{4,2,1,3,0:T(8,128)(2,1)}, u32[]{:S(2)}, u32[]{:S(2)}) collective-permute-start(bf16[2,4,64,4,256]{4,2,1,3,0:T(8,128)(2,1)} %get-tuple-element.120), channel_id=1, source_target_pairs={{0,4},{4,8},{8,12},{12,16},{16,20},{20,24},{24,28},{28,32},{32,36}... | collective-permute-start | bytes 3145736 | tf_op jit(solution)/shard_map/ppermute | solution.py:17
  185.2 3.8 %slice.61 = bf16[2,8,64,4,1,128]{5,4,3,2,1,0:T(2,128)(2,1)S(1)} slice(bf16[2,8,64,4,3,128]{5,4,3,2,1,0:T(4,128)(2,1)} %reshape.107), slice={[0:2], [0:8], [0:64], [0:4], [0:1], [0:128]} | slice | bytes 2097152 | tf_op jit(solution)/shard_map/slice | solution.py:57
  189.3 37.8 %collective-permute-done.6 = bf16[2,4,64,4,256]{4,2,1,3,0:T(8,128)(2,1)} collective-permute-done((bf16[2,4,64,4,256]{4,2,1,3,0:T(8,128)(2,1)}, bf16[2,4,64,4,256]{4,2,1,3,0:T(8,128)(2,1)}, u32[]{:S(2)}, u32[]{:S(2)}) %collective-permute-start.6) | collective-permute-done | bytes 1048608 | tf_op jit(solution)/shard_map/ppermute | solution.py:17
  227.0 4.6 %collective-permute-done.7 = bf16[2,4,64,4,256]{4,2,1,3,0:T(8,128)(2,1)} collective-permute-done((bf16[2,4,64,4,256]{4,2,1,3,0:T(8,128)(2,1)}, bf16[2,4,64,4,256]{4,2,1,3,0:T(8,128)(2,1)}, u32[]{:S(2)}, u32[]{:S(2)}) %collective-permute-start.7) | collective-permute-done | bytes 1048608 | tf_op jit(solution)/shard_map/ppermute | solution.py:19
  231.7 3.4 %pad_maximum_fusion = bf16[2,16,64,4,256]{4,2,1,3,0:T(8,128)(2,1)} fusion(bf16[2,4,64,4,256]{4,2,1,3,0:T(8,128)(2,1)} %collective-permute-done.7, bf16[2,8,64,4,256]{4,2,1,3,0:T(8,128)(2,1)S(1)} %copy.48, bf16[2,4,64,4,256]{4,2,1,3,0:T(8,128)(2,1)} %collective-permute-done.6), kind=kLoop, calls=%fused_computation.25 | loop fusion | flops 4194304 | bytes 8388608 | tf_op jit(solution)/shard_map/concatenate | solution.py:15
  235.0 44.8 %while.12 = (s32[]{:T(128)}, bf16[2,2,4,64,4,128]{5,3,4,2,0,1:T(8,128)(2,1)}, s32[2]{0:T(128)S(1)}, bf16[2,16,64,4,256]{4,2,1,3,0:T(8,128)(2,1)}, s32[]{:T(128)}...) while((s32[]{:T(128)}, ...), condition=%wide.region_4.5_spmd, body=%wide.region_1.4_spmd.sunk | while | flops 824439104 | bytes 64005228 | solution.py:86
  236.3 3.7 %fusion.49 = (f32[2,4,4,64]{3,2,1,0:T(4,128)S(1)}, f32[2,4,4,64,12,64]{3,5,4,2,1,0:T(8,128)S(1)}) fusion(pred[4,12]{1,0:T(4,128)(4,1)S(1)} %fusion.48, bf16[2,16,64,4,256]{4,2,1,3,0:T(8,128)(2,1)} %get-tuple-element.200, s32[]{:T(128)S(6)} %select_n.43, bf16[2,8,64,4,128]{4,2,1,3,0:T(8,128)(2,1)S(1)} %get-tuple-element.202, s32[]{:T(128)S(6)} %select_n.44), kind=kOutput, calls=%fused_computation.3.clone.1 | convolution fusion | flops 407369728 | bytes 8397320 | tf_op jit(solution)/shard_map/while/body/eval_jaxpr/tiahd,tjbhd->thiajb/dot_general | solution.py:70
  240.0 4.5 %copy-done.2 = f32[2,4,4,64,12,64]{3,5,4,2,1,0:T(8,128)} copy-done((f32[2,4,4,64,12,64]{3,5,4,2,1,0:T(8,128)}, f32[2,4,4,64,12,64]{3,5,4,2,1,0:T(8,128)S(1)}, u32[]{:S(2)}) %copy-start.2) | copy-done | bytes 6291480 | tf_op jit(solution)/shard_map/while
  244.6 3.4 %fusion.50 = f32[2,4,4,64]{3,2,1,0:T(4,128)S(1)} fusion(f32[2,4,4,64,12,64]{3,5,4,2,1,0:T(8,128)S(1)} %get-tuple-element.171, f32[2,4,4,64]{3,2,1,0:T(4,128)S(1)} %get-tuple-element.172, pred[4,12]{1,0:T(4,128)(4,1)S(1)} %fusion.48), kind=kLoop, calls=%fused_computation.4.clone.1 | loop fusion | flops 6289408 | bytes 6307888 | tf_op jit(solution)/shard_map/while/body/eval_jaxpr/reduce_sum | solution.py:80
  248.0 8.4 %fusion.51 = bf16[1,2,4,64,4,128]{5,3,2,4,1,0:T(8,128)(2,1)S(1)} fusion(f32[2,4,4,64,12,64]{3,5,4,2,1,0:T(8,128)} %copy-done.2, f32[2,4,4,64]{3,2,1,0:T(4,128)S(1)} %fusion.50, f32[2,4,4,64]{3,2,1,0:T(4,128)S(1)} %get-tuple-element.172, pred[4,12]{1,0:T(4,128)(4,1)S(1)} %fusion.48, bf16[2,16,64,4,256]{4,2,1,3,0:T(8,128)(2,1)} %get-tuple-element.200, ...), kind=kOutput, calls=%fused_computation.11.clone.1 | convolution fusion | flops 410779648 | bytes 14696504 | tf_op jit(solution)/shard_map/while/body/eval_jaxpr/thiajb,tjbhd->tiahd/dot_general | solution.py:81
  258.7 3.7 %fusion.49 = (f32[2,4,4,64]{3,2,1,0:T(4,128)S(1)}, f32[2,4,4,64,12,64]{3,5,4,2,1,0:T(8,128)S(1)}) fusion(pred[4,12]{1,0:T(4,128)(4,1)S(1)} %fusion.48, bf16[2,16,64,4,256]{4,2,1,3,0:T(8,128)(2,1)} %get-tuple-element.200, s32[]{:T(128)S(6)} %select_n.43, bf16[2,8,64,4,128]{4,2,1,3,0:T(8,128)(2,1)S(1)} %get-tuple-element.202, s32[]{:T(128)S(6)} %select_n.44), kind=kOutput, calls=%fused_computation.3.clone.1 | convolution fusion | flops 407369728 | bytes 8397320 | tf_op jit(solution)/shard_map/while/body/eval_jaxpr/tiahd,tjbhd->thiajb/dot_general | solution.py:70
  262.4 4.5 %copy-done.2 = f32[2,4,4,64,12,64]{3,5,4,2,1,0:T(8,128)} copy-done((f32[2,4,4,64,12,64]{3,5,4,2,1,0:T(8,128)}, f32[2,4,4,64,12,64]{3,5,4,2,1,0:T(8,128)S(1)}, u32[]{:S(2)}) %copy-start.2) | copy-done | bytes 6291480 | tf_op jit(solution)/shard_map/while
  267.0 3.4 %fusion.50 = f32[2,4,4,64]{3,2,1,0:T(4,128)S(1)} fusion(f32[2,4,4,64,12,64]{3,5,4,2,1,0:T(8,128)S(1)} %get-tuple-element.171, f32[2,4,4,64]{3,2,1,0:T(4,128)S(1)} %get-tuple-element.172, pred[4,12]{1,0:T(4,128)(4,1)S(1)} %fusion.48), kind=kLoop, calls=%fused_computation.4.clone.1 | loop fusion | flops 6289408 | bytes 6307888 | tf_op jit(solution)/shard_map/while/body/eval_jaxpr/reduce_sum | solution.py:80
  270.4 8.4 %fusion.51 = bf16[1,2,4,64,4,128]{5,3,2,4,1,0:T(8,128)(2,1)S(1)} fusion(f32[2,4,4,64,12,64]{3,5,4,2,1,0:T(8,128)} %copy-done.2, f32[2,4,4,64]{3,2,1,0:T(4,128)S(1)} %fusion.50, f32[2,4,4,64]{3,2,1,0:T(4,128)S(1)} %get-tuple-element.172, pred[4,12]{1,0:T(4,128)(4,1)S(1)} %fusion.48, bf16[2,16,64,4,256]{4,2,1,3,0:T(8,128)(2,1)} %get-tuple-element.200, ...), kind=kOutput, calls=%fused_computation.11.clone.1 | convolution fusion | flops 410779648 | bytes 14696504 | tf_op jit(solution)/shard_map/while/body/eval_jaxpr/thiajb,tjbhd->tiahd/dot_general | solution.py:81
  282.3 4.2 %all-to-all-start = ((bf16[2,8,64,4,128]{4,2,1,0,3:T(8,128)(2,1)}), bf16[2,8,64,4,128]{4,2,1,0,3:T(8,128)(2,1)}, u32[]{:S(2)}, u32[]{:S(2)}) async-start(bf16[2,8,64,4,128]{4,2,1,0,3:T(8,128)(2,1)} %copy.54), calls=%async_computation | async-start | bytes 2097152 | tf_op jit(solution)/shard_map/all_to_all | solution.py:90
  288.5 12.7 %all-to-all-done = bf16[2,8,64,4,128]{4,2,1,0,3:T(8,128)(2,1)} async-done(((bf16[2,8,64,4,128]{4,2,1,0,3:T(8,128)(2,1)}), bf16[2,8,64,4,128]{4,2,1,0,3:T(8,128)(2,1)}, u32[]{:S(2)}, u32[]{:S(2)}) %all-to-all-start) | async-done | bytes 1048608 | tf_op jit(solution)/shard_map/all_to_all | solution.py:90
  (61 shorter events, 34.4 us)
Async XLA Ops:
  7.2 45.4 %copy-start = (bf16[3,3,3,256,256]{4,3,2,1,0:T(8,128)(2,1)S(1)}, bf16[3,3,3,256,256]{4,3,2,1,0:T(8,128)(2,1)}, u32[]{:S(2)}) copy-start(bf16[3,3,3,256,256]{4,3,2,1,0:T(8,128)(2,1)} %param.8) | copy-start | bytes 10616836
  7.2 99.1 %all-gather.3.cloned.1.call-start = ((), (), s32[]{:S(2)}) async-start(), calls=%async_computation.1 | async-start | bytes 2621440 | tf_op jit(solution)/shard_map/all_gather | solution.py:46
  10.4 8.2 %collective-permute-start = (bf16[1,16,32,256]{3,1,2,0:T(8,128)(2,1)S(1)}, bf16[1,16,32,256]{3,1,2,0:T(8,128)(2,1)S(1)}, u32[]{:S(2)}, u32[]{:S(2)}) collective-permute-start(bf16[1,16,32,256]{3,1,2,0:T(8,128)(2,1)S(1)} %get-tuple-element.126), channel_id=1, source_target_pairs={{0,64},{64,128},{128,192},{1,65},{65,129},{129,193},{2,66},{66,130... | collective-permute-start | bytes 786440 | tf_op jit(solution)/shard_map/ppermute | solution.py:17
  13.6 8.8 %collective-permute-start.1 = (bf16[1,16,32,256]{3,1,2,0:T(8,128)(2,1)S(1)}, bf16[1,16,32,256]{3,1,2,0:T(8,128)(2,1)S(1)}, u32[]{:S(2)}, u32[]{:S(2)}) collective-permute-start(bf16[1,16,32,256]{3,1,2,0:T(8,128)(2,1)S(1)} %get-tuple-element.127), channel_id=1, source_target_pairs={{64,0},{128,64},{192,128},{65,1},{129,65},{193,129},{66,2},{130,66... | collective-permute-start | bytes 786440 | tf_op jit(solution)/shard_map/ppermute | solution.py:19
  22.6 11.2 %collective-permute-start.2 = (bf16[4,1,32,256]{3,1,2,0:T(2,128)(2,1)S(1)}, bf16[4,1,32,256]{3,1,2,0:T(2,128)(2,1)S(1)}, u32[]{:S(2)}, u32[]{:S(2)}) collective-permute-start(bf16[4,1,32,256]{3,1,2,0:T(2,128)(2,1)S(1)} %get-tuple-element.124), channel_id=1, source_target_pairs={{0,4},{4,8},{8,12},{12,16},{16,20},{20,24},{24,28},{28,32},{32,36}... | collective-permute-start | bytes 196616 | tf_op jit(solution)/shard_map/ppermute | solution.py:17
  31.4 11.6 %collective-permute-start.3 = (bf16[4,1,32,256]{3,1,2,0:T(2,128)(2,1)S(1)}, bf16[4,1,32,256]{3,1,2,0:T(2,128)(2,1)S(1)}, u32[]{:S(2)}, u32[]{:S(2)}) collective-permute-start(bf16[4,1,32,256]{3,1,2,0:T(2,128)(2,1)S(1)} %get-tuple-element.125), channel_id=1, source_target_pairs={{4,0},{8,4},{12,8},{16,12},{20,16},{24,20},{28,24},{32,28},{36,32}... | collective-permute-start | bytes 196616 | tf_op jit(solution)/shard_map/ppermute | solution.py:19
  43.0 5.3 %collective-permute-start.4 = (bf16[4,18,1,256]{3,1,2,0:T(8,128)(2,1)S(1)}, bf16[4,18,1,256]{3,1,2,0:T(8,128)(2,1)S(1)}, u32[]{:S(2)}, u32[]{:S(2)}) collective-permute-start(bf16[4,18,1,256]{3,1,2,0:T(8,128)(2,1)S(1)} %get-tuple-element.122), channel_id=1, source_target_pairs={{0,1},{1,2},{2,3},{4,5},{5,6},{6,7},{8,9},{9,10},{10,11},{12,13},{... | collective-permute-start | bytes 110600 | tf_op jit(solution)/shard_map/ppermute | solution.py:17
  44.9 4.8 %collective-permute-start.5 = (bf16[4,18,1,256]{3,1,2,0:T(8,128)(2,1)S(1)}, bf16[4,18,1,256]{3,1,2,0:T(8,128)(2,1)S(1)}, u32[]{:S(2)}, u32[]{:S(2)}) collective-permute-start(bf16[4,18,1,256]{3,1,2,0:T(8,128)(2,1)S(1)} %get-tuple-element.123), channel_id=1, source_target_pairs={{1,0},{2,1},{3,2},{5,4},{6,5},{7,6},{9,8},{10,9},{11,10},{13,12},{... | collective-permute-start | bytes 110600 | tf_op jit(solution)/shard_map/ppermute | solution.py:19
  51.5 1.1 copy-start.6
  52.6 5.4 %copy-start.3 = (bf16[2,16,32,256]{3,2,1,0:T(8,128)(2,1)S(1)}, bf16[2,16,32,256]{3,2,1,0:T(8,128)(2,1)}, u32[]{:S(2)}) copy-start(bf16[2,16,32,256]{3,2,1,0:T(8,128)(2,1)} %param.6) | copy-start | bytes 1572868
  59.2 91.5 %all-gather.5.cloned.1.call-start = ((), (), s32[]{:S(2)}) async-start(), calls=%async_computation.2 | async-start | bytes 3932160 | tf_op jit(solution)/shard_map/all_gather | solution.py:44
  176.7 50.3 %collective-permute-start.6 = (bf16[2,4,64,4,256]{4,2,1,3,0:T(8,128)(2,1)}, bf16[2,4,64,4,256]{4,2,1,3,0:T(8,128)(2,1)}, u32[]{:S(2)}, u32[]{:S(2)}) collective-permute-start(bf16[2,4,64,4,256]{4,2,1,3,0:T(8,128)(2,1)} %get-tuple-element.120), channel_id=1, source_target_pairs={{0,4},{4,8},{8,12},{12,16},{16,20},{20,24},{24,28},{28,32},{32,36}... | collective-permute-start | bytes 3145736 | tf_op jit(solution)/shard_map/ppermute | solution.py:17
  183.0 48.6 %collective-permute-start.7 = (bf16[2,4,64,4,256]{4,2,1,3,0:T(8,128)(2,1)}, bf16[2,4,64,4,256]{4,2,1,3,0:T(8,128)(2,1)}, u32[]{:S(2)}, u32[]{:S(2)}) collective-permute-start(bf16[2,4,64,4,256]{4,2,1,3,0:T(8,128)(2,1)} %get-tuple-element.121), channel_id=1, source_target_pairs={{4,0},{8,4},{12,8},{16,12},{20,16},{24,20},{28,24},{32,28},{36,32}... | collective-permute-start | bytes 3145736 | tf_op jit(solution)/shard_map/ppermute | solution.py:19
  240.0 4.5 %copy-start.2 = (f32[2,4,4,64,12,64]{3,5,4,2,1,0:T(8,128)}, f32[2,4,4,64,12,64]{3,5,4,2,1,0:T(8,128)S(1)}, u32[]{:S(2)}) copy-start(f32[2,4,4,64,12,64]{3,5,4,2,1,0:T(8,128)S(1)} %get-tuple-element.171) | copy-start | bytes 18874372 | tf_op jit(solution)/shard_map/while
  248.0 8.4 %copy-start.4 = (bf16[2,2,4,64,4,128]{5,3,4,2,0,1:T(8,128)(2,1)S(1)}, bf16[2,2,4,64,4,128]{5,3,4,2,0,1:T(8,128)(2,1)}, u32[]{:S(2)}) copy-start(bf16[2,2,4,64,4,128]{5,3,4,2,0,1:T(8,128)(2,1)} %get-tuple-element.186) | copy-start | bytes 3145732 | tf_op jit(solution)/shard_map/while
  256.5 1.0 copy-start.5
  262.4 4.5 %copy-start.2 = (f32[2,4,4,64,12,64]{3,5,4,2,1,0:T(8,128)}, f32[2,4,4,64,12,64]{3,5,4,2,1,0:T(8,128)S(1)}, u32[]{:S(2)}) copy-start(f32[2,4,4,64,12,64]{3,5,4,2,1,0:T(8,128)S(1)} %get-tuple-element.171) | copy-start | bytes 18874372 | tf_op jit(solution)/shard_map/while
  270.4 8.4 %copy-start.4 = (bf16[2,2,4,64,4,128]{5,3,4,2,0,1:T(8,128)(2,1)S(1)}, bf16[2,2,4,64,4,128]{5,3,4,2,0,1:T(8,128)(2,1)}, u32[]{:S(2)}) copy-start(bf16[2,2,4,64,4,128]{5,3,4,2,0,1:T(8,128)(2,1)} %get-tuple-element.186) | copy-start | bytes 3145732 | tf_op jit(solution)/shard_map/while
  278.9 1.0 copy-start.5
  279.9 23.7 %copy-start.1 = (bf16[3,3,3,256,256]{4,3,2,1,0:T(8,128)(2,1)S(1)}, bf16[3,3,3,256,256]{4,3,2,1,0:T(8,128)(2,1)}, u32[]{:S(2)}) copy-start(bf16[3,3,3,256,256]{4,3,2,1,0:T(8,128)(2,1)} %param.8) | copy-start | bytes 10616836
  282.3 19.0 %all-to-all-start = ((bf16[2,8,64,4,128]{4,2,1,0,3:T(8,128)(2,1)}), bf16[2,8,64,4,128]{4,2,1,0,3:T(8,128)(2,1)}, u32[]{:S(2)}, u32[]{:S(2)}) async-start(bf16[2,8,64,4,128]{4,2,1,0,3:T(8,128)(2,1)} %copy.54), calls=%async_computation | async-start | bytes 2097152 | tf_op jit(solution)/shard_map/all_to_all | solution.py:90
Sparse Core Ops, SparseCore 0:
  59.3 46.8 all-gather.2
  108.1 42.5 all-gather.4
where the time goes:
time: 311 us; the launch traced here: 310 us
  waiting for transfers between devices  154 us (50%)
  local copies, waits for them, and re-layouts  56 us (18%)
  matrix products  35.1 us (11%)
  starting transfers between devices  33.3 us (11%)
  other arithmetic  15.9 us (5%)
  between operations  14.3 us (5%)
    all_gather x1, waiting for transfers between devices, local(): wide = lax.all_gather(block_out, 'wa', axis=2, tiled=True)  46.3 us
    ppermute x4, waiting for transfers between devices, extended(): lax.ppermute(tail, axis, [(i, (i + 1) % count) for i in range(ends)])  42 us
    all_gather x1, waiting for transfers between devices, local(): col_heads = lax.all_gather(qkv_weight, 'ta', axis=1, tiled=True)  33.7 us
    ppermute x4, starting transfers between devices, extended(): lax.ppermute(tail, axis, [(i, (i + 1) % count) for i in range(ends)])  20.1 us
    ppermute x4, waiting for transfers between devices, extended(): lax.ppermute(head, axis, [((i + 1) % count, i) for i in range(ends)])  19 us
    dot_general x2, matrix products, attend(): jnp.einsum('thiajb,tjbhd->tiahd', probs, value_part, preferred_element_ty...  16.7 us
    all_to_all x1, waiting for transfers between devices, local(): lax.all_to_all(attended, 'ta', split_axis=3, concat_axis=0, tiled=True)  12.7 us
    while x12, local copies, waits for them, and re-layouts  11 us
  transfers between devices with their start and end apart: 11, of which 10 were waited for; matrix products, arithmetic and copies ran while one was open for 5% of the time, Pallas kernels for 0%

commit v1 on v0

--- a/solution.py
+++ b/solution.py
@@ -41,7 +41,9 @@
     )[0]
     block_out = (latent_f32 + conv_out).astype(jnp.bfloat16)
     width_in, head_dev, qkv_count, head_size = qkv_weight.shape
-    col_heads = lax.all_gather(qkv_weight, "ta", axis=1, tiled=True)
+    col_heads = jnp.concatenate(
+        lax.all_to_all(jnp.stack([qkv_weight] * lax.axis_size("ta")), "ta", 0, 0), axis=1
+    )
     heads = col_heads.shape[1]
     wide = lax.all_gather(block_out, "wa", axis=2, tiled=True)
     patch_cols = wide.shape[2] // 2

time: 311 us -> 274 us (0.88)
  the two profiles are of different devices: /device:TPU:67 before, /device:TPU:5 now
where the time goes in v1:
time: 274 us
  waiting for transfers between devices  114 us (42%)
  local copies, waits for them, and re-layouts  53.8 us (20%)
  starting transfers between devices  38.8 us (14%)
  matrix products  35.1 us (13%)
  other arithmetic  15.9 us (6%)
  between operations  14.3 us (5%)
    ppermute x4, waiting for transfers between devices, extended(): lax.ppermute(tail, axis, [(i, (i + 1) % count) for i in range(ends)])  43.3 us
    all_gather x1, waiting for transfers between devices, local(): wide = lax.all_gather(block_out, 'wa', axis=2, tiled=True)  39.3 us
    ppermute x4, starting transfers between devices, extended(): lax.ppermute(tail, axis, [(i, (i + 1) % count) for i in range(ends)])  23.1 us
    ppermute x4, waiting for transfers between devices, extended(): lax.ppermute(head, axis, [((i + 1) % count, i) for i in range(ends)])  19.1 us
    dot_general x2, matrix products, attend(): jnp.einsum('thiajb,tjbhd->tiahd', probs, value_part, preferred_element_ty...  16.7 us
    all_to_all x1, waiting for transfers between devices, local(): lax.all_to_all(attended, 'ta', split_axis=3, concat_axis=0, tiled=True)  12.4 us
    while x12, local copies, waits for them, and re-layouts  11 us
    dot_general x2, matrix products, attend(): jnp.einsum('tiahd,tjbhd->thiajb', q_block, key_part, preferred_element_ty...  7.39 us
  transfers between devices with their start and end apart: 11, of which 9 were waited for; matrix products, arithmetic and copies ran while one was open for 7% of the time, Pallas kernels for 0%

profile of v1, /device:TPU:5, one launch (start us, length us, event | category | flops | bytes accessed | tf_op | source)
XLA Modules:
  0.0 273.6 jit_solution(14102131641881272047)
XLA Ops:
  10.4 3.2 %collective-permute-start = (bf16[1,16,32,256]{3,1,2,0:T(8,128)(2,1)S(1)}, bf16[1,16,32,256]{3,1,2,0:T(8,128)(2,1)S(1)}, u32[]{:S(2)}, u32[]{:S(2)}) collective-permute-start(bf16[1,16,32,256]{3,1,2,0:T(8,128)(2,1)S(1)} %get-tuple-element.126), channel_id=1, source_target_pairs={{0,64},{64,128},{128,192},{1,65},{65,129},{129,193},{2,66},{66,130... | collective-permute-start | bytes 786440 | tf_op jit(solution)/shard_map/ppermute | solution.py:17
  14.9 3.7 %collective-permute-done = bf16[1,16,32,256]{3,1,2,0:T(8,128)(2,1)S(1)} collective-permute-done((bf16[1,16,32,256]{3,1,2,0:T(8,128)(2,1)S(1)}, bf16[1,16,32,256]{3,1,2,0:T(8,128)(2,1)S(1)}, u32[]{:S(2)}, u32[]{:S(2)}) %collective-permute-start) | collective-permute-done | bytes 262176 | tf_op jit(solution)/shard_map/ppermute | solution.py:17
  18.6 3.8 %collective-permute-done.1 = bf16[1,16,32,256]{3,1,2,0:T(8,128)(2,1)S(1)} collective-permute-done((bf16[1,16,32,256]{3,1,2,0:T(8,128)(2,1)S(1)}, bf16[1,16,32,256]{3,1,2,0:T(8,128)(2,1)S(1)}, u32[]{:S(2)}, u32[]{:S(2)}) %collective-permute-start.1) | collective-permute-done | bytes 262176 | tf_op jit(solution)/shard_map/ppermute | solution.py:19
  22.6 10.5 %collective-permute-start.2 = (bf16[4,1,32,256]{3,1,2,0:T(2,128)(2,1)S(1)}, bf16[4,1,32,256]{3,1,2,0:T(2,128)(2,1)S(1)}, u32[]{:S(2)}, u32[]{:S(2)}) collective-permute-start(bf16[4,1,32,256]{3,1,2,0:T(2,128)(2,1)S(1)} %get-tuple-element.124), channel_id=1, source_target_pairs={{0,4},{4,8},{8,12},{12,16},{16,20},{20,24},{24,28},{28,32},{32,36}... | collective-permute-start | bytes 196616 | tf_op jit(solution)/shard_map/ppermute | solution.py:17
  37.3 6.1 %collective-permute-done.3 = bf16[4,1,32,256]{3,1,2,0:T(2,128)(2,1)S(1)} collective-permute-done((bf16[4,1,32,256]{3,1,2,0:T(2,128)(2,1)S(1)}, bf16[4,1,32,256]{3,1,2,0:T(2,128)(2,1)S(1)}, u32[]{:S(2)}, u32[]{:S(2)}) %collective-permute-start.3) | collective-permute-done | bytes 65568 | tf_op jit(solution)/shard_map/ppermute | solution.py:19
  47.4 4.2 %collective-permute-done.5 = bf16[4,18,1,256]{3,1,2,0:T(8,128)(2,1)S(1)} collective-permute-done((bf16[4,18,1,256]{3,1,2,0:T(8,128)(2,1)S(1)}, bf16[4,18,1,256]{3,1,2,0:T(8,128)(2,1)S(1)}, u32[]{:S(2)}, u32[]{:S(2)}) %collective-permute-start.5) | collective-permute-done | bytes 36896 | tf_op jit(solution)/shard_map/ppermute | solution.py:19
  54.4 5.0 %fusion.23 = f32[2,16,8,5,256]{4,2,3,1,0:T(8,128)S(1)} fusion(bf16[3,3,3,256,256]{4,3,2,1,0:T(8,128)(2,1)S(1)} %copy-done, bf16[4,18,1,7,2,256]{5,3,4,1,0,2:T(8,128)(2,1)S(1)} %slice.56, bf16[4,18,1,8,5,256]{5,3,4,1,0,2:T(8,128)(2,1)S(1)} %copy.45, pred[8,5]{0,1:T(8,128)(4,1)S(1)} %copy-done.7), kind=kOutput, calls=%fused_computation.40 | convolution fusion | flops 4536369152 | bytes 6840360 | tf_op jit(solution)/shard_map/conv_general_dilated | solution.py:34
  63.4 4.8 %all-to-all-start = ((bf16[4,1024,1,3,128]{1,4,3,2,0:T(8,128)(2,1)}), bf16[4,1024,1,3,128]{1,4,3,2,0:T(8,128)(2,1)}, u32[]{:S(2)}, u32[]{:S(2)}) async-start(bf16[4,1024,1,3,128]{1,4,3,2,0:T(8,128)(2,1)} %stack.2), calls=%async_computation | async-start | bytes 6291456 | tf_op jit(solution)/shard_map/all_to_all | solution.py:45
  68.3 39.3 %all-gather.2.cloned.1.call-done = bf16[2,16,128,256]{3,1,2,0:T(8,128)(2,1)} async-done(((bf16[2,16,32,256]{3,1,2,0:T(8,128)(2,1)}), bf16[2,16,128,256]{3,1,2,0:T(8,128)(2,1)}) %all-gather.2.cloned.1.call-update) | async-done | bytes 2097168 | tf_op jit(solution)/shard_map/all_gather | solution.py:48
  107.6 2.7 %reshape.107 = bf16[2,8,2,64,2,256]{5,2,1,4,3,0:T(2,128)(2,1)S(1)} reshape(bf16[2,16,128,256]{3,1,2,0:T(8,128)(2,1)} %all-gather.2.cloned.1.call-done) | data formatting | bytes 4194304 | tf_op jit(solution)/shard_map/reshape | solution.py:51
  110.3 3.6 %copy.76 = bf16[2,8,2,64,2,256]{5,4,2,3,1,0:T(2,128)(2,1)} copy(bf16[2,8,2,64,2,256]{5,2,1,4,3,0:T(2,128)(2,1)S(1)} %reshape.107) | data formatting | bytes 4194304 | tf_op jit(solution)/shard_map/reshape | solution.py:51
  113.9 4.5 %reshape.108 = bf16[1024,1024]{1,0:T(8,128)(2,1)} reshape(bf16[2,8,64,2,2,256]{5,4,3,2,1,0:T(2,128)(2,1)} %bitcast.93) | data formatting | bytes 4194304 | tf_op jit(solution)/shard_map/reshape | solution.py:53
  118.4 6.0 %convolution_convert_fusion = bf16[1024,1536]{1,0:T(8,128)(2,1)S(1)} fusion(bf16[1024,1024]{1,0:T(8,128)(2,1)} %reshape.108, bf16[1024,1536]{0,1:T(8,128)(2,1)} %bitcast.20), kind=kOutput, calls=%fused_computation.28 | convolution fusion | flops 3222798336 | bytes 8388608 | tf_op jit(solution)/shard_map/dot_general | solution.py:55
  124.4 4.5 %reshape.110 = bf16[2,8,64,4,3,128]{5,4,3,2,1,0:T(4,128)(2,1)} reshape(bf16[1024,1536]{1,0:T(8,128)(2,1)S(1)} %convolution_convert_fusion) | data formatting | bytes 6291456 | tf_op jit(solution)/shard_map/reshape | solution.py:58
  128.9 4.6 %slice.58 = bf16[2,8,64,4,2,128]{5,4,3,2,1,0:T(2,128)(2,1)S(1)} slice(bf16[2,8,64,4,3,128]{5,4,3,2,1,0:T(4,128)(2,1)} %reshape.110), slice={[0:2], [0:8], [0:64], [0:4], [1:3], [0:128]} | slice | bytes 4194304 | tf_op jit(solution)/shard_map/slice | solution.py:60
  133.5 2.6 reshape.111
  139.8 6.7 %collective-permute-start.6 = (bf16[2,4,64,4,256]{4,2,1,3,0:T(8,128)(2,1)}, bf16[2,4,64,4,256]{4,2,1,3,0:T(8,128)(2,1)}, u32[]{:S(2)}, u32[]{:S(2)}) collective-permute-start(bf16[2,4,64,4,256]{4,2,1,3,0:T(8,128)(2,1)} %get-tuple-element.120), channel_id=1, source_target_pairs={{0,4},{4,8},{8,12},{12,16},{16,20},{20,24},{24,28},{28,32},{32,36}... | collective-permute-start | bytes 3145736 | tf_op jit(solution)/shard_map/ppermute | solution.py:17
  148.7 3.8 %slice.61 = bf16[2,8,64,4,1,128]{5,4,3,2,1,0:T(2,128)(2,1)S(1)} slice(bf16[2,8,64,4,3,128]{5,4,3,2,1,0:T(4,128)(2,1)} %reshape.110), slice={[0:2], [0:8], [0:64], [0:4], [0:1], [0:128]} | slice | bytes 2097152 | tf_op jit(solution)/shard_map/slice | solution.py:59
  152.7 37.4 %collective-permute-done.6 = bf16[2,4,64,4,256]{4,2,1,3,0:T(8,128)(2,1)} collective-permute-done((bf16[2,4,64,4,256]{4,2,1,3,0:T(8,128)(2,1)}, bf16[2,4,64,4,256]{4,2,1,3,0:T(8,128)(2,1)}, u32[]{:S(2)}, u32[]{:S(2)}) %collective-permute-start.6) | collective-permute-done | bytes 1048608 | tf_op jit(solution)/shard_map/ppermute | solution.py:17
  190.2 5.0 %collective-permute-done.7 = bf16[2,4,64,4,256]{4,2,1,3,0:T(8,128)(2,1)} collective-permute-done((bf16[2,4,64,4,256]{4,2,1,3,0:T(8,128)(2,1)}, bf16[2,4,64,4,256]{4,2,1,3,0:T(8,128)(2,1)}, u32[]{:S(2)}, u32[]{:S(2)}) %collective-permute-start.7) | collective-permute-done | bytes 1048608 | tf_op jit(solution)/shard_map/ppermute | solution.py:19
  195.1 3.4 %pad_maximum_fusion = bf16[2,16,64,4,256]{4,2,1,3,0:T(8,128)(2,1)} fusion(bf16[2,4,64,4,256]{4,2,1,3,0:T(8,128)(2,1)} %collective-permute-done.7, bf16[2,8,64,4,256]{4,2,1,3,0:T(8,128)(2,1)S(1)} %copy.50, bf16[2,4,64,4,256]{4,2,1,3,0:T(8,128)(2,1)} %collective-permute-done.6), kind=kLoop, calls=%fused_computation.25 | loop fusion | flops 4194304 | bytes 8388608 | tf_op jit(solution)/shard_map/concatenate | solution.py:15
  198.5 44.8 %while.12 = (s32[]{:T(128)}, bf16[2,2,4,64,4,128]{5,3,4,2,0,1:T(8,128)(2,1)}, s32[2]{0:T(128)S(1)}, bf16[2,16,64,4,256]{4,2,1,3,0:T(8,128)(2,1)}, s32[]{:T(128)}...) while((s32[]{:T(128)}, ...), condition=%wide.region_4.5_spmd, body=%wide.region_1.4_spmd.sunk | while | flops 824439104 | bytes 64005228 | solution.py:88
  199.8 3.7 %fusion.49 = (f32[2,4,4,64]{3,2,1,0:T(4,128)S(1)}, f32[2,4,4,64,12,64]{3,5,4,2,1,0:T(8,128)S(1)}) fusion(pred[4,12]{1,0:T(4,128)(4,1)S(1)} %fusion.48, bf16[2,16,64,4,256]{4,2,1,3,0:T(8,128)(2,1)} %get-tuple-element.200, s32[]{:T(128)S(6)} %select_n.43, bf16[2,8,64,4,128]{4,2,1,3,0:T(8,128)(2,1)S(1)} %get-tuple-element.202, s32[]{:T(128)S(6)} %select_n.44), kind=kOutput, calls=%fused_computation.3.clone.1 | convolution fusion | flops 407369728 | bytes 8397320 | tf_op jit(solution)/shard_map/while/body/eval_jaxpr/tiahd,tjbhd->thiajb/dot_general | solution.py:72
  203.5 4.5 %copy-done.2 = f32[2,4,4,64,12,64]{3,5,4,2,1,0:T(8,128)} copy-done((f32[2,4,4,64,12,64]{3,5,4,2,1,0:T(8,128)}, f32[2,4,4,64,12,64]{3,5,4,2,1,0:T(8,128)S(1)}, u32[]{:S(2)}) %copy-start.2) | copy-done | bytes 6291480 | tf_op jit(solution)/shard_map/while
  208.0 3.4 %fusion.50 = f32[2,4,4,64]{3,2,1,0:T(4,128)S(1)} fusion(f32[2,4,4,64,12,64]{3,5,4,2,1,0:T(8,128)S(1)} %get-tuple-element.171, f32[2,4,4,64]{3,2,1,0:T(4,128)S(1)} %get-tuple-element.172, pred[4,12]{1,0:T(4,128)(4,1)S(1)} %fusion.48), kind=kLoop, calls=%fused_computation.4.clone.1 | loop fusion | flops 6289408 | bytes 6307888 | tf_op jit(solution)/shard_map/while/body/eval_jaxpr/reduce_sum | solution.py:82
  211.5 8.4 %fusion.51 = bf16[1,2,4,64,4,128]{5,3,2,4,1,0:T(8,128)(2,1)S(1)} fusion(f32[2,4,4,64,12,64]{3,5,4,2,1,0:T(8,128)} %copy-done.2, f32[2,4,4,64]{3,2,1,0:T(4,128)S(1)} %fusion.50, f32[2,4,4,64]{3,2,1,0:T(4,128)S(1)} %get-tuple-element.172, pred[4,12]{1,0:T(4,128)(4,1)S(1)} %fusion.48, bf16[2,16,64,4,256]{4,2,1,3,0:T(8,128)(2,1)} %get-tuple-element.200, ...), kind=kOutput, calls=%fused_computation.11.clone.1 | convolution fusion | flops 410779648 | bytes 14696504 | tf_op jit(solution)/shard_map/while/body/eval_jaxpr/thiajb,tjbhd->tiahd/dot_general | solution.py:83
  222.2 3.7 %fusion.49 = (f32[2,4,4,64]{3,2,1,0:T(4,128)S(1)}, f32[2,4,4,64,12,64]{3,5,4,2,1,0:T(8,128)S(1)}) fusion(pred[4,12]{1,0:T(4,128)(4,1)S(1)} %fusion.48, bf16[2,16,64,4,256]{4,2,1,3,0:T(8,128)(2,1)} %get-tuple-element.200, s32[]{:T(128)S(6)} %select_n.43, bf16[2,8,64,4,128]{4,2,1,3,0:T(8,128)(2,1)S(1)} %get-tuple-element.202, s32[]{:T(128)S(6)} %select_n.44), kind=kOutput, calls=%fused_computation.3.clone.1 | convolution fusion | flops 407369728 | bytes 8397320 | tf_op jit(solution)/shard_map/while/body/eval_jaxpr/tiahd,tjbhd->thiajb/dot_general | solution.py:72
  225.9 4.5 %copy-done.2 = f32[2,4,4,64,12,64]{3,5,4,2,1,0:T(8,128)} copy-done((f32[2,4,4,64,12,64]{3,5,4,2,1,0:T(8,128)}, f32[2,4,4,64,12,64]{3,5,4,2,1,0:T(8,128)S(1)}, u32[]{:S(2)}) %copy-start.2) | copy-done | bytes 6291480 | tf_op jit(solution)/shard_map/while
  230.4 3.4 %fusion.50 = f32[2,4,4,64]{3,2,1,0:T(4,128)S(1)} fusion(f32[2,4,4,64,12,64]{3,5,4,2,1,0:T(8,128)S(1)} %get-tuple-element.171, f32[2,4,4,64]{3,2,1,0:T(4,128)S(1)} %get-tuple-element.172, pred[4,12]{1,0:T(4,128)(4,1)S(1)} %fusion.48), kind=kLoop, calls=%fused_computation.4.clone.1 | loop fusion | flops 6289408 | bytes 6307888 | tf_op jit(solution)/shard_map/while/body/eval_jaxpr/reduce_sum | solution.py:82
  233.9 8.4 %fusion.51 = bf16[1,2,4,64,4,128]{5,3,2,4,1,0:T(8,128)(2,1)S(1)} fusion(f32[2,4,4,64,12,64]{3,5,4,2,1,0:T(8,128)} %copy-done.2, f32[2,4,4,64]{3,2,1,0:T(4,128)S(1)} %fusion.50, f32[2,4,4,64]{3,2,1,0:T(4,128)S(1)} %get-tuple-element.172, pred[4,12]{1,0:T(4,128)(4,1)S(1)} %fusion.48, bf16[2,16,64,4,256]{4,2,1,3,0:T(8,128)(2,1)} %get-tuple-element.200, ...), kind=kOutput, calls=%fused_computation.11.clone.1 | convolution fusion | flops 410779648 | bytes 14696504 | tf_op jit(solution)/shard_map/while/body/eval_jaxpr/thiajb,tjbhd->tiahd/dot_general | solution.py:83
  245.8 4.2 %all-to-all-start.1 = ((bf16[2,8,64,4,128]{4,2,1,0,3:T(8,128)(2,1)}), bf16[2,8,64,4,128]{4,2,1,0,3:T(8,128)(2,1)}, u32[]{:S(2)}, u32[]{:S(2)}) async-start(bf16[2,8,64,4,128]{4,2,1,0,3:T(8,128)(2,1)} %copy.56), calls=%async_computation.1 | async-start | bytes 2097152 | tf_op jit(solution)/shard_map/all_to_all | solution.py:92
  252.0 12.4 %all-to-all-done.1 = bf16[2,8,64,4,128]{4,2,1,0,3:T(8,128)(2,1)} async-done(((bf16[2,8,64,4,128]{4,2,1,0,3:T(8,128)(2,1)}), bf16[2,8,64,4,128]{4,2,1,0,3:T(8,128)(2,1)}, u32[]{:S(2)}, u32[]{:S(2)}) %all-to-all-start.1) | async-done | bytes 1048608 | tf_op jit(solution)/shard_map/all_to_all | solution.py:92
  (63 shorter events, 35.6 us)
Async XLA Ops:
  7.2 47.2 %copy-start = (bf16[3,3,3,256,256]{4,3,2,1,0:T(8,128)(2,1)S(1)}, bf16[3,3,3,256,256]{4,3,2,1,0:T(8,128)(2,1)}, u32[]{:S(2)}) copy-start(bf16[3,3,3,256,256]{4,3,2,1,0:T(8,128)(2,1)} %param.8) | copy-start | bytes 10616836
  7.2 100.4 %all-gather.2.cloned.1.call-start = ((), (), s32[]{:S(2)}) async-start(), calls=%async_computation.2 | async-start | bytes 2621440 | tf_op jit(solution)/shard_map/all_gather | solution.py:48
  10.4 8.2 %collective-permute-start = (bf16[1,16,32,256]{3,1,2,0:T(8,128)(2,1)S(1)}, bf16[1,16,32,256]{3,1,2,0:T(8,128)(2,1)S(1)}, u32[]{:S(2)}, u32[]{:S(2)}) collective-permute-start(bf16[1,16,32,256]{3,1,2,0:T(8,128)(2,1)S(1)} %get-tuple-element.126), channel_id=1, source_target_pairs={{0,64},{64,128},{128,192},{1,65},{65,129},{129,193},{2,66},{66,130... | collective-permute-start | bytes 786440 | tf_op jit(solution)/shard_map/ppermute | solution.py:17
  13.6 8.8 %collective-permute-start.1 = (bf16[1,16,32,256]{3,1,2,0:T(8,128)(2,1)S(1)}, bf16[1,16,32,256]{3,1,2,0:T(8,128)(2,1)S(1)}, u32[]{:S(2)}, u32[]{:S(2)}) collective-permute-start(bf16[1,16,32,256]{3,1,2,0:T(8,128)(2,1)S(1)} %get-tuple-element.127), channel_id=1, source_target_pairs={{64,0},{128,64},{192,128},{65,1},{129,65},{193,129},{66,2},{130,66... | collective-permute-start | bytes 786440 | tf_op jit(solution)/shard_map/ppermute | solution.py:19
  22.6 14.7 %collective-permute-start.2 = (bf16[4,1,32,256]{3,1,2,0:T(2,128)(2,1)S(1)}, bf16[4,1,32,256]{3,1,2,0:T(2,128)(2,1)S(1)}, u32[]{:S(2)}, u32[]{:S(2)}) collective-permute-start(bf16[4,1,32,256]{3,1,2,0:T(2,128)(2,1)S(1)} %get-tuple-element.124), channel_id=1, source_target_pairs={{0,4},{4,8},{8,12},{12,16},{16,20},{20,24},{24,28},{28,32},{32,36}... | collective-permute-start | bytes 196616 | tf_op jit(solution)/shard_map/ppermute | solution.py:17
  33.1 10.3 %collective-permute-start.3 = (bf16[4,1,32,256]{3,1,2,0:T(2,128)(2,1)S(1)}, bf16[4,1,32,256]{3,1,2,0:T(2,128)(2,1)S(1)}, u32[]{:S(2)}, u32[]{:S(2)}) collective-permute-start(bf16[4,1,32,256]{3,1,2,0:T(2,128)(2,1)S(1)} %get-tuple-element.125), channel_id=1, source_target_pairs={{4,0},{8,4},{12,8},{16,12},{20,16},{24,20},{28,24},{32,28},{36,32}... | collective-permute-start | bytes 196616 | tf_op jit(solution)/shard_map/ppermute | solution.py:19
  43.5 3.9 %collective-permute-start.4 = (bf16[4,18,1,256]{3,1,2,0:T(8,128)(2,1)S(1)}, bf16[4,18,1,256]{3,1,2,0:T(8,128)(2,1)S(1)}, u32[]{:S(2)}, u32[]{:S(2)}) collective-permute-start(bf16[4,18,1,256]{3,1,2,0:T(8,128)(2,1)S(1)} %get-tuple-element.122), channel_id=1, source_target_pairs={{0,1},{1,2},{2,3},{4,5},{5,6},{6,7},{8,9},{9,10},{10,11},{12,13},{... | collective-permute-start | bytes 110600 | tf_op jit(solution)/shard_map/ppermute | solution.py:17
  46.1 5.5 %collective-permute-start.5 = (bf16[4,18,1,256]{3,1,2,0:T(8,128)(2,1)S(1)}, bf16[4,18,1,256]{3,1,2,0:T(8,128)(2,1)S(1)}, u32[]{:S(2)}, u32[]{:S(2)}) collective-permute-start(bf16[4,18,1,256]{3,1,2,0:T(8,128)(2,1)S(1)} %get-tuple-element.123), channel_id=1, source_target_pairs={{1,0},{2,1},{3,2},{5,4},{6,5},{7,6},{9,8},{10,9},{11,10},{13,12},{... | collective-permute-start | bytes 110600 | tf_op jit(solution)/shard_map/ppermute | solution.py:19
  53.3 1.1 copy-start.7
  54.4 5.4 %copy-start.3 = (bf16[2,16,32,256]{3,2,1,0:T(8,128)(2,1)S(1)}, bf16[2,16,32,256]{3,2,1,0:T(8,128)(2,1)}, u32[]{:S(2)}) copy-start(bf16[2,16,32,256]{3,2,1,0:T(8,128)(2,1)} %param.6) | copy-start | bytes 1572868
  59.4 1.6 copy-start.6
  63.4 54.9 %all-to-all-start = ((bf16[4,1024,1,3,128]{1,4,3,2,0:T(8,128)(2,1)}), bf16[4,1024,1,3,128]{1,4,3,2,0:T(8,128)(2,1)}, u32[]{:S(2)}, u32[]{:S(2)}) async-start(bf16[4,1024,1,3,128]{1,4,3,2,0:T(8,128)(2,1)} %stack.2), calls=%async_computation | async-start | bytes 6291456 | tf_op jit(solution)/shard_map/all_to_all | solution.py:45
  139.8 50.4 %collective-permute-start.6 = (bf16[2,4,64,4,256]{4,2,1,3,0:T(8,128)(2,1)}, bf16[2,4,64,4,256]{4,2,1,3,0:T(8,128)(2,1)}, u32[]{:S(2)}, u32[]{:S(2)}) collective-permute-start(bf16[2,4,64,4,256]{4,2,1,3,0:T(8,128)(2,1)} %get-tuple-element.120), channel_id=1, source_target_pairs={{0,4},{4,8},{8,12},{12,16},{16,20},{20,24},{24,28},{28,32},{32,36}... | collective-permute-start | bytes 3145736 | tf_op jit(solution)/shard_map/ppermute | solution.py:17
  146.5 48.6 %collective-permute-start.7 = (bf16[2,4,64,4,256]{4,2,1,3,0:T(8,128)(2,1)}, bf16[2,4,64,4,256]{4,2,1,3,0:T(8,128)(2,1)}, u32[]{:S(2)}, u32[]{:S(2)}) collective-permute-start(bf16[2,4,64,4,256]{4,2,1,3,0:T(8,128)(2,1)} %get-tuple-element.121), channel_id=1, source_target_pairs={{4,0},{8,4},{12,8},{16,12},{20,16},{24,20},{28,24},{32,28},{36,32}... | collective-permute-start | bytes 3145736 | tf_op jit(solution)/shard_map/ppermute | solution.py:19
  203.5 4.5 %copy-start.2 = (f32[2,4,4,64,12,64]{3,5,4,2,1,0:T(8,128)}, f32[2,4,4,64,12,64]{3,5,4,2,1,0:T(8,128)S(1)}, u32[]{:S(2)}) copy-start(f32[2,4,4,64,12,64]{3,5,4,2,1,0:T(8,128)S(1)} %get-tuple-element.171) | copy-start | bytes 18874372 | tf_op jit(solution)/shard_map/while
  211.5 8.4 %copy-start.4 = (bf16[2,2,4,64,4,128]{5,3,4,2,0,1:T(8,128)(2,1)S(1)}, bf16[2,2,4,64,4,128]{5,3,4,2,0,1:T(8,128)(2,1)}, u32[]{:S(2)}) copy-start(bf16[2,2,4,64,4,128]{5,3,4,2,0,1:T(8,128)(2,1)} %get-tuple-element.186) | copy-start | bytes 3145732 | tf_op jit(solution)/shard_map/while
  220.0 1.0 copy-start.5
  225.9 4.5 %copy-start.2 = (f32[2,4,4,64,12,64]{3,5,4,2,1,0:T(8,128)}, f32[2,4,4,64,12,64]{3,5,4,2,1,0:T(8,128)S(1)}, u32[]{:S(2)}) copy-start(f32[2,4,4,64,12,64]{3,5,4,2,1,0:T(8,128)S(1)} %get-tuple-element.171) | copy-start | bytes 18874372 | tf_op jit(solution)/shard_map/while
  233.9 8.4 %copy-start.4 = (bf16[2,2,4,64,4,128]{5,3,4,2,0,1:T(8,128)(2,1)S(1)}, bf16[2,2,4,64,4,128]{5,3,4,2,0,1:T(8,128)(2,1)}, u32[]{:S(2)}) copy-start(bf16[2,2,4,64,4,128]{5,3,4,2,0,1:T(8,128)(2,1)} %get-tuple-element.186) | copy-start | bytes 3145732 | tf_op jit(solution)/shard_map/while
  242.4 1.0 copy-start.5
  243.3 23.4 %copy-start.1 = (bf16[3,3,3,256,256]{4,3,2,1,0:T(8,128)(2,1)S(1)}, bf16[3,3,3,256,256]{4,3,2,1,0:T(8,128)(2,1)}, u32[]{:S(2)}) copy-start(bf16[3,3,3,256,256]{4,3,2,1,0:T(8,128)(2,1)} %param.8) | copy-start | bytes 10616836
  245.8 18.7 %all-to-all-start.1 = ((bf16[2,8,64,4,128]{4,2,1,0,3:T(8,128)(2,1)}), bf16[2,8,64,4,128]{4,2,1,0,3:T(8,128)(2,1)}, u32[]{:S(2)}, u32[]{:S(2)}) async-start(bf16[2,8,64,4,128]{4,2,1,0,3:T(8,128)(2,1)} %copy.56), calls=%async_computation.1 | async-start | bytes 2097152 | tf_op jit(solution)/shard_map/all_to_all | solution.py:92
Sparse Core Ops, SparseCore 0:
  61.2 46.3 all-gather.1
